TPU v7x, 32 devices: a whole 2x2x4 slice. The times are simulated.
32 devices in a mesh: groups: 2 (over y), cls: 4 (over z), img: 4 (over x, core).
Axes of the slice: x: 2, y: 2, z: 4, core: 2. Of those that a mesh axis runs over, the one named last changes fastest.
Arguments:
- particles: bfloat16 [512, 2, 4608], P(('groups', 'img', 'cls')), parts along dimension 0, may hold values from -30 to 30
- classes: bfloat16 [256, 2, 4608], P(('groups', 'cls')), parts along dimension 0, may hold values from -4 to 4
- ctf: float32 [128, 4608], P('groups'), parts along dimension 0, may hold values from 0.1 to 1
- noise_weight: float32 [9216], P('groups'), parts along dimension 0, may hold values from 0.01 to 0.1
- group_ids: int32 [512], P(('groups', 'img', 'cls')), parts along dimension 0, may hold values from 0 to 63
- shifts: int32 [48, 2], P('groups'), parts along dimension 0, may hold values from -6 to 6
Outputs:
- log_resp: float32 [512, 128], P(('groups', 'img'), 'cls'), parts along dimension 0
- averages: float32 [256, 2, 4608], P(('groups', 'cls'), None, 'img'), parts along dimension 0
There are 2 independent parts, one for each index of `groups`. A program takes and returns all parts, laid end to end along the dimension named above; each array names one. Nothing has to cross between parts.
All inputs are finite; a program needn't handle non-finite values.
Results may differ from a plain program's by a relative error of at most 0.012.
The roundings to bfloat16 on the way count: a program that leaves them out, or rounds other values in their place, can miss the bound.
Values may be sent and summed in bfloat16 or wider, within the bound.
A program may use at most 128 MiB of HBM per device.

v0:
```python
import jax
import jax.numpy as jnp
from jax import lax
from jax.sharding import PartitionSpec as P

BOX = 128
prior_precision = 0.02


def phase_tables(shifts, freq):
    index = jnp.arange(freq)
    along_y = (index // BOX).astype(jnp.float32)
    along_x = (index % BOX - BOX // 2).astype(jnp.float32)
    angle = (
        2.0
        * jnp.pi
        / BOX
        * (
            shifts[:, 0:1].astype(jnp.float32) * along_x[None, :]
            + shifts[:, 1:2].astype(jnp.float32) * along_y[None, :]
        )
    )
    return (jnp.cos(angle), jnp.sin(angle))


def local(particles, classes, ctf, noise_weight, group_ids, shifts):
    part_rows = particles.shape[0]
    freq = particles.shape[2]
    cls_rows = classes.shape[0]
    poses = shifts.shape[0]
    groups = ctf.shape[0]
    total_rows = part_rows * lax.axis_size("cls")
    cos_t, sin_t = phase_tables(shifts, freq)
    real_part = classes[:, 0, :].astype(jnp.float32)
    imag_part = classes[:, 1, :].astype(jnp.float32)
    temp_re = real_part[None] * cos_t[:, None, :] - imag_part[None] * sin_t[:, None, :]
    temp_im = real_part[None] * sin_t[:, None, :] + imag_part[None] * cos_t[:, None, :]
    templates = (
        jnp.stack([temp_re, temp_im], axis=2)
        .astype(jnp.bfloat16)
        .reshape(poses * cls_rows, 2 * freq)
    )
    marks_local = (group_ids[:, None] == jnp.arange(groups)[None, :]).astype(jnp.float32)
    selected = jnp.dot(marks_local, ctf, precision=lax.Precision.HIGHEST)
    weighted = (
        particles.astype(jnp.float32) * (selected * noise_weight[None, :])[:, None, :]
    ).astype(jnp.bfloat16)
    weighted = weighted.reshape(part_rows, 2 * freq)
    marks_low = marks_local.astype(jnp.bfloat16)
    ctf_weight = ctf * ctf * noise_weight[None, :]
    power = jnp.dot(
        ctf_weight,
        (real_part * real_part + imag_part * imag_part).T,
        precision=lax.Precision.HIGHEST,
    )
    gathered, marks_all = (
        lax.all_gather(weighted, "cls", axis=0, tiled=True),
        lax.all_gather(marks_low, "cls", axis=0, tiled=True),
    )
    cross = lax.dot_general(
        gathered, templates, (((1,), (1,)), ((), ())), preferred_element_type=jnp.float32
    )
    penalty = jnp.dot(marks_all.astype(jnp.float32), power, precision=lax.Precision.HIGHEST)
    scores = cross.reshape(gathered.shape[0], poses, cls_rows) - 0.5 * penalty[:, None, :]
    local_peak = jnp.max(scores, axis=(1, 2))
    peak = lax.pmax(local_peak, "cls")
    total = lax.psum(jnp.sum(jnp.exp(scores - peak[:, None, None]), axis=(1, 2)), "cls")
    log_norm = peak + jnp.log(total)
    pose_peak = jnp.max(scores, axis=1)
    log_resp = (
        pose_peak
        + jnp.log(jnp.sum(jnp.exp(scores - pose_peak[:, None, :]), axis=1))
        - log_norm[:, None]
    )
    rho = jnp.exp(scores - log_norm[:, None, None])
    rho_low = rho.astype(jnp.bfloat16).reshape(total_rows, poses * cls_rows)
    pose_total = jnp.sum(rho, axis=1)
    sums = lax.dot_general(
        rho_low, gathered, (((0,), (0,)), ((), ())), preferred_element_type=jnp.float32
    )
    mass_table = jnp.dot(
        pose_total.T, marks_all.astype(jnp.float32), precision=lax.Precision.HIGHEST
    )
    sums = sums.reshape(poses, cls_rows, 2, freq)
    cos_b = cos_t[:, None, :]
    sin_b = sin_t[:, None, :]
    numer_re = jnp.sum(sums[:, :, 0, :] * cos_b + sums[:, :, 1, :] * sin_b, axis=0)
    numer_im = jnp.sum(sums[:, :, 1, :] * cos_b - sums[:, :, 0, :] * sin_b, axis=0)
    numer = jnp.stack([numer_re, numer_im], axis=1)
    denom = jnp.dot(mass_table, ctf_weight, precision=lax.Precision.HIGHEST)
    numer_part, denom_part = (
        lax.psum_scatter(numer, "img", scatter_dimension=2, tiled=True),
        lax.psum_scatter(denom, "img", scatter_dimension=1, tiled=True),
    )
    averages = numer_part / (denom_part[:, None, :] + prior_precision)
    return (log_resp, averages)


def solution(mesh):
    placed = (
        P(("groups", "img", "cls"), None, None),
        P(("groups", "cls"), None, None),
        P("groups", None),
        P("groups"),
        P(("groups", "img", "cls")),
        P("groups", None),
    )
    return jax.shard_map(
        local,
        mesh=mesh,
        in_specs=placed,
        out_specs=(P(("groups", "img"), "cls"), P(("groups", "cls"), None, "img")),
        check_vma=False,
    )
```

profile of v0, /device:TPU:0, one launch (start us, length us, event | category | flops | bytes accessed | tf_op | source)
XLA Modules:
  0.0 220.5 jit_solution(17909339871494409727)
XLA Ops:
  7.2 1.8 convolution_multiply_fusion
  9.0 1.3 multiply_convert_fusion
  10.3 0.7 copy.26
  11.0 0.0 reduce-scatter.5.cloned.1.call-start
  11.1 2.4 %fusion.34 = (bf16[32,1,4608]{2,1,0:T(2,128)(2,1)S(1)}, bf16[32,1,4608]{2,1,0:T(2,128)(2,1)S(1)}) fusion(bf16[32,2,4608]{2,1,0:T(2,128)(2,1)} %param.7), kind=kLoop, calls=%fused_computation.61 | loop fusion | bytes 1179648 | tf_op jit(solution)/shard_map/slice | solution.py:34
  13.5 0.8 convert_bitcast_fusion.1
  14.3 0.1 fusion.18
  14.3 1.6 fusion.15
  16.0 30.8 %subtract_convert_fusion = (bf16[24,32,1,4608]{3,2,1,0:T(2,128)(2,1)S(1)}, bf16[24,32,1,4608]{3,2,1,0:T(2,128)(2,1)}) fusion(f32[24,4608]{1,0:T(8,128)S(1)} %get-tuple-element.17, f32[32,4608]{1,0:T(8,128)S(1)} %get-tuple-element.22, f32[24,4608]{1,0:T(8,128)S(1)} %get-tuple-element.16, f32[32,4608]{1,0:T(8,128)S(1)} %get-tuple-element.23), kind=kLoop, calls=%fused_computation.6 | loop fusion | flops 28311552 | bytes 16220160 | tf_op jit(solution)/shard_map/convert.2
  46.8 34.8 %pad_maximum_fusion = bf16[24,32,2,4608]{3,2,1,0:T(2,128)(2,1)} fusion(bf16[24,32,1,4608]{3,2,1,0:T(2,128)(2,1)} %get-tuple-element.13, bf16[24,32,1,4608]{3,2,1,0:T(2,128)(2,1)S(1)} %get-tuple-element.12), kind=kLoop, calls=%fused_computation.2 | loop fusion | flops 28311552 | bytes 28311552 | tf_op jit(solution)/shard_map/stack | solution.py:39
  81.6 22.7 %convert_element_type.73 = bf16[24,32,9216]{2,1,0:T(8,128)(2,1)} reshape(bf16[24,32,2,4608]{3,2,1,0:T(2,128)(2,1)} %pad_maximum_fusion) | data formatting | bytes 28311552 | tf_op jit(solution)/shard_map/convert_element_type | solution.py:40
  104.3 0.1 convert_convert_fusion
  104.4 14.8 %all_gather.7 = bf16[64,64]{1,0:T(8,128)(2,1)S(1)} all-gather(bf16[16,64]{1,0:T(8,128)(2,1)S(1)} %convert_convert_fusion), channel_id=1, replica_groups=mesh['groups'=2,'cls'=4,'img'=4] {'cls'}, dimensions={0}, use_global_device_ids=true | all-gather | bytes 10240 | tf_op jit(solution)/shard_map/all_gather | solution.py:58
  119.2 1.2 fusion.8
  120.4 0.1 convolution_multiply_fusion.1
  120.5 0.0 all-gather.2.cloned.1.call-done
  120.6 7.5 %fusion.35 = (f32[64]{0:T(128)S(1)}, f32[64,24,32]{0,2,1:T(8,128)S(1)}) fusion(f32[64,32]{0,1:T(8,128)S(1)} %convolution_multiply_fusion.1, bf16[24,32,9216]{2,1,0:T(8,128)(2,1)} %convert_element_type.73, bf16[64,9216]{1,0:T(8,128)(2,1)} %all-gather.2.cloned.1.call-done), kind=kOutput, calls=%fused_computation.62 | convolution fusion | flops 906067904 | bytes 15540480 | tf_op jit(solution)/shard_map/dot_general | solution.py:60
  128.1 11.7 %pmax.7 = f32[64]{0:T(128)S(1)} all-reduce(f32[64]{0:T(128)S(1)} %get-tuple-element.20), channel_id=1, replica_groups=mesh['groups'=2,'cls'=4,'img'=4] {'cls'}, use_global_device_ids=true, to_apply=%region_3.4 | all-reduce | flops 64 | bytes 512 | tf_op jit(solution)/shard_map/pmax | solution.py:66
  139.8 0.1 exponential_reduce_fusion
  139.9 8.5 %psum.7 = f32[64]{0:T(128)S(1)} all-reduce(f32[64]{0:T(128)S(1)} %get-tuple-element.10), channel_id=1, replica_groups=mesh['groups'=2,'cls'=4,'img'=4] {'cls'}, use_global_device_ids=true, to_apply=%region_5.6 | all-reduce | flops 64 | bytes 512 | tf_op jit(solution)/shard_map/psum | solution.py:67
  148.5 0.1 fusion.16
  148.6 11.4 %fusion = f32[24,32,2,4608]{3,1,2,0:T(8,128)} fusion(bf16[8,2,8,4608]{3,2,1,0:T(8,128)(2,1)S(1)} %bitcast.71, f32[64,24,32]{0,2,1:T(8,128)S(1)} %get-tuple-element.21, f32[64]{0:T(128)S(1)} %log_add_fusion), kind=kOutput, calls=%fused_computation.9 | convolution fusion | flops 906067968 | bytes 29688064 | tf_op jit(solution)/shard_map/dot_general | solution.py:78
  160.1 0.1 fusion.36
  160.2 1.6 fusion.7
  161.8 10.9 %add_reduce_fusion = (f32[32,4608]{1,0:T(8,128)S(1)}, f32[32,4608]{1,0:T(8,128)S(1)}) fusion(f32[24,32,2,4608]{3,1,2,0:T(8,128)} %fusion, f32[24,4608]{1,0:T(8,128)} %copy-done.2, f32[24,4608]{1,0:T(8,128)S(1)} %get-tuple-element.16), kind=kLoop, calls=%fused_computation.4 | loop fusion | flops 28016640 | bytes 30375936 | tf_op jit(solution)/shard_map/reduce_sum | solution.py:87
  172.8 1.1 pad_maximum_fusion.1
  173.9 0.6 add_subtract_fusion
  174.5 9.2 %reduce-scatter.5.cloned.1.call-done = f32[32,1152]{1,0:T(8,128)} async-done(((f32[32,4608]{1,0:T(8,128)}), f32[32,1152]{1,0:T(8,128)}) %reduce-scatter.5.cloned.1.call-update) | async-done | bytes 147472 | tf_op jit(solution)/shard_map/reduce_scatter | solution.py:93
  183.7 0.9 broadcast_add_fusion
  184.6 27.4 %reduce-scatter.3.cloned.1.call-done = f32[32,2,1152]{2,0,1:T(8,128)} async-done(((f32[32,2,4608]{2,0,1:T(8,128)}), f32[32,2,1152]{2,0,1:T(8,128)}) %reduce-scatter.3.cloned.1.call-update) | async-done | bytes 294928 | tf_op jit(solution)/shard_map/reduce_scatter | solution.py:92
  212.0 1.0 broadcast_divide_fusion
  213.0 0.9 copy.20
  (17 shorter events, 0.2 us)
Async XLA Ops:
  7.2 113.4 %all-gather.2.cloned.1.call-start = ((), (), s32[]{:S(2)}) async-start(), calls=%async_computation.2 | async-start | bytes 1474560 | tf_op jit(solution)/shard_map/all_gather | solution.py:57
  11.0 172.6 %reduce-scatter.5.cloned.1.call-start = ((), (), s32[]{:S(2)}) async-start(), calls=%async_computation.4 | async-start | bytes 737280 | tf_op jit(solution)/shard_map/reduce_scatter | solution.py:93
  16.0 30.8 %copy-start.2 = (f32[24,4608]{1,0:T(8,128)}, f32[24,4608]{1,0:T(8,128)S(1)}, u32[]{:S(2)}) copy-start(f32[24,4608]{1,0:T(8,128)S(1)} %get-tuple-element.17) | copy-start | bytes 1327108
  81.6 22.7 %copy-start.4 = (s32[16]{0:T(128)S(1)}, s32[16]{0:T(128)}, u32[]{:S(2)}) copy-start(s32[16]{0:T(128)} %param.10) | copy-start | bytes 196
  81.6 37.6 %copy-start = (f32[64,4608]{1,0:T(8,128)S(1)}, f32[64,4608]{1,0:T(8,128)}, u32[]{:S(2)}) copy-start(f32[64,4608]{1,0:T(8,128)} %param.8) | copy-start | bytes 3538948
  81.6 37.6 %copy-start.3 = (f32[4608]{0:T(1024)S(1)}, f32[4608]{0:T(1024)}, u32[]{:S(2)}) copy-start(f32[4608]{0:T(1024)} %param.9) | copy-start | bytes 55300
  120.6 28.1 %copy-start.1 = (bf16[64,9216]{1,0:T(8,128)(2,1)S(1)}, bf16[64,9216]{1,0:T(8,128)(2,1)}, u32[]{:S(2)}) copy-start(bf16[64,9216]{1,0:T(8,128)(2,1)} %all-gather.2.cloned.1.call-done) | copy-start | bytes 3538948
  161.8 50.2 %reduce-scatter.3.cloned.1.call-start = ((), (), s32[]{:S(2)}) async-start(), calls=%async_computation.3 | async-start | bytes 1474560 | tf_op jit(solution)/shard_map/reduce_scatter | solution.py:92
Sparse Core Ops, SparseCore 0:
  11.2 33.1 all-gather.1
  161.9 21.7 reduce-scatter.4
  186.3 25.7 reduce-scatter.2
where the time goes:
time: 221 us; the launch traced here: 220 us
  other arithmetic  84.3 us (38%)
  waiting for transfers between devices  36.7 us (17%)
  blocking collectives  35.1 us (16%)
  local copies, waits for them, and re-layouts  26.8 us (12%)
  matrix products  23.7 us (11%)
  between operations  13.9 us (6%)
    another operation x1, other arithmetic, local(): jnp.stack([temp_re, temp_im], axis=2).astype(jnp.bfloat16)  34.8 us
    another operation x1, other arithmetic  30.8 us
    reduce_scatter x1, waiting for transfers between devices, local(): lax.psum_scatter(numer, 'img', scatter_dimension=2, tiled=True)  27.4 us
    convert_element_type x1, local copies, waits for them, and re-layouts, local(): templates = jnp.stack([temp_re, temp_im], axis=2).astype(jnp.bfloat16).re...  22.7 us
    all_gather x1, blocking collectives, local(): lax.all_gather(marks_low, 'cls', axis=0, tiled=True)  14.8 us
    pmax x1, blocking collectives, local(): peak = lax.pmax(local_peak, 'cls')  11.7 us
    dot_general x1, matrix products, local(): lax.dot_general(rho_low, gathered, (((0,), (0,)), ((), ())), preferred_el...  11.4 us
    reduce_sum x1, other arithmetic, local(): jnp.sum(sums[:, :, 0, :] * cos_b + sums[:, :, 1, :] * sin_b, axis=0)  10.9 us
  transfers between devices with their start and end apart: 3, of which 2 were waited for; matrix products, arithmetic and copies ran while one was open for 49% of the time, Pallas kernels for 0%

commit v1 on v0

--- a/solution.py
+++ b/solution.py
@@ -5,6 +5,18 @@
 
 BOX = 128
 prior_precision = 0.02
+
+
+def doubled_up(x, axis, dim):
+    ways, here = (lax.axis_size(axis), lax.axis_index(axis))
+    grown, reach = (x, 1)
+    while reach < ways:
+        theirs = lax.ppermute(grown, axis, [(d, d ^ reach) for d in range(ways)])
+        mine_first = jnp.concatenate([grown, theirs], axis=dim)
+        theirs_first = jnp.concatenate([theirs, grown], axis=dim)
+        grown = jnp.where(here & reach == 0, mine_first, theirs_first)
+        reach = 2 * reach
+    return grown
 
 
 def phase_tables(shifts, freq):
@@ -55,7 +67,7 @@
     )
     gathered, marks_all = (
         lax.all_gather(weighted, "cls", axis=0, tiled=True),
-        lax.all_gather(marks_low, "cls", axis=0, tiled=True),
+        doubled_up(marks_low, "cls", 0),
     )
     cross = lax.dot_general(
         gathered, templates, (((1,), (1,)), ((), ())), preferred_element_type=jnp.float32

time: 221 us -> 210 us (0.950)
  blocking collectives: 35.1 us -> 18.9 us
  starting transfers between devices: 0.12 us -> 5.8 us
    all_gather x1 -> x0, blocking collectives: 14.8 us -> none  [local(): lax.all_gather(marks_low, 'cls', axis=0, tiled=True)]
    ppermute x0 -> x2, starting transfers between devices: none -> 5.68 us  [doubled_up(): theirs = lax.ppermute(grown, axis, [(d, d ^ reach) for d in range(ways)])]
    pmax x1, blocking collectives: 11.7 us -> 8.82 us  [local(): peak = lax.pmax(local_peak, 'cls')]
  transfers between devices with their start and end apart: 3 -> 5, of which waited for: 2 -> 2; matrix products, arithmetic and copies ran while one was open for 49% -> 53% of each run, Pallas kernels for 0% -> 0%
where the time goes in v1:
time: 210 us; the launch traced here: 209 us
  other arithmetic  85.1 us (41%)
  waiting for transfers between devices  35.2 us (17%)
  local copies, waits for them, and re-layouts  26.7 us (13%)
  matrix products  23.7 us (11%)
  blocking collectives  18.9 us (9%)
  between operations  13.9 us (7%)
  starting transfers between devices  5.8 us (3%)
    another operation x1, other arithmetic, local(): jnp.stack([temp_re, temp_im], axis=2).astype(jnp.bfloat16)  34.9 us
    another operation x1, other arithmetic  30.8 us
    reduce_scatter x1, waiting for transfers between devices, local(): lax.psum_scatter(numer, 'img', scatter_dimension=2, tiled=True)  27.4 us
    convert_element_type x1, local copies, waits for them, and re-layouts, local(): templates = jnp.stack([temp_re, temp_im], axis=2).astype(jnp.bfloat16).re...  22.6 us
    dot_general x1, matrix products, local(): lax.dot_general(rho_low, gathered, (((0,), (0,)), ((), ())), preferred_el...  11.4 us
    reduce_sum x1, other arithmetic, local(): jnp.sum(sums[:, :, 0, :] * cos_b + sums[:, :, 1, :] * sin_b, axis=0)  10.9 us
    psum x1, blocking collectives, local(): lax.psum(jnp.sum(jnp.exp(scores - peak[:, None, None]), axis=(1, 2)), 'cls')  10.1 us
    pmax x1, blocking collectives, local(): peak = lax.pmax(local_peak, 'cls')  8.82 us
  transfers between devices with their start and end apart: 5, of which 2 were waited for; matrix products, arithmetic and copies ran while one was open for 53% of the time, Pallas kernels for 0%

profile of v1, /device:TPU:0, one launch (start us, length us, event | category | flops | bytes accessed | tf_op | source)
XLA Modules:
  0.0 209.2 jit_solution(1938288387920021132)
XLA Ops:
  7.2 0.7 convert_convert_fusion
  7.9 3.0 %collective-permute-start = (bf16[16,64]{1,0:T(8,128)(2,1)S(1)}, bf16[16,64]{1,0:T(8,128)(2,1)S(1)}, u32[]{:S(2)}, u32[]{:S(2)}) collective-permute-start(bf16[16,64]{1,0:T(8,128)(2,1)S(1)} %convert_convert_fusion), channel_id=1, source_target_pairs={{0,4},{4,0},{8,12},{12,8},{1,5},{5,1},{9,13},{13,9},{2,6},{6,2},{1... | collective-permute-start | bytes 6152 | tf_op jit(solution)/shard_map/ppermute | solution.py:14
  11.0 1.8 convolution_multiply_fusion
  12.7 1.3 multiply_convert_fusion
  14.0 0.7 copy.26
  14.9 2.4 %fusion.37 = (bf16[32,1,4608]{2,1,0:T(2,128)(2,1)S(1)}, bf16[32,1,4608]{2,1,0:T(2,128)(2,1)S(1)}) fusion(bf16[32,2,4608]{2,1,0:T(2,128)(2,1)} %param.7), kind=kLoop, calls=%fused_computation.66 | loop fusion | bytes 1179648 | tf_op jit(solution)/shard_map/slice | solution.py:46
  17.2 0.8 convert_bitcast_fusion.1
  18.0 0.1 fusion.18
  18.1 1.6 fusion.15
  19.7 30.8 %subtract_convert_fusion = (bf16[24,32,1,4608]{3,2,1,0:T(2,128)(2,1)S(1)}, bf16[24,32,1,4608]{3,2,1,0:T(2,128)(2,1)}) fusion(f32[24,4608]{1,0:T(8,128)S(1)} %get-tuple-element.17, f32[32,4608]{1,0:T(8,128)S(1)} %get-tuple-element.22, f32[24,4608]{1,0:T(8,128)S(1)} %get-tuple-element.16, f32[32,4608]{1,0:T(8,128)S(1)} %get-tuple-element.23), kind=kLoop, calls=%fused_computation.6 | loop fusion | flops 28311552 | bytes 16220160 | tf_op jit(solution)/shard_map/convert.2
  50.6 34.9 %pad_maximum_fusion = bf16[24,32,2,4608]{3,2,1,0:T(2,128)(2,1)} fusion(bf16[24,32,1,4608]{3,2,1,0:T(2,128)(2,1)} %get-tuple-element.13, bf16[24,32,1,4608]{3,2,1,0:T(2,128)(2,1)S(1)} %get-tuple-element.12), kind=kLoop, calls=%fused_computation.2 | loop fusion | flops 28311552 | bytes 28311552 | tf_op jit(solution)/shard_map/stack | solution.py:51
  85.5 2.7 %collective-permute-start.1 = (bf16[32,64]{1,0:T(8,128)(2,1)S(1)}, bf16[32,64]{1,0:T(8,128)(2,1)S(1)}, u32[]{:S(2)}, u32[]{:S(2)}) collective-permute-start(bf16[32,64]{1,0:T(8,128)(2,1)S(1)} %maximum_select_fusion.1), channel_id=1, source_target_pairs={{0,8},{4,12},{8,0},{12,4},{1,9},{5,13},{9,1},{13,5},{2,10},{6,14},... | collective-permute-start | bytes 12296 | tf_op jit(solution)/shard_map/ppermute | solution.py:14
  88.2 1.2 fusion.8
  89.3 22.6 %convert_element_type.73 = bf16[24,32,9216]{2,1,0:T(8,128)(2,1)} reshape(bf16[24,32,2,4608]{3,2,1,0:T(2,128)(2,1)} %pad_maximum_fusion) | data formatting | bytes 28311552 | tf_op jit(solution)/shard_map/convert_element_type | solution.py:52
  111.9 0.1 convolution_multiply_fusion.1
  112.1 7.5 %fusion.38 = (f32[64]{0:T(128)S(1)}, f32[64,24,32]{0,2,1:T(8,128)S(1)}) fusion(f32[64,32]{0,1:T(8,128)S(1)} %convolution_multiply_fusion.1, bf16[24,32,9216]{2,1,0:T(8,128)(2,1)} %convert_element_type.73, bf16[64,9216]{1,0:T(8,128)(2,1)} %all-gather.2.cloned.1.call-done), kind=kOutput, calls=%fused_computation.67 | convolution fusion | flops 906067904 | bytes 15540480 | tf_op jit(solution)/shard_map/dot_general | solution.py:72
  119.6 8.8 %pmax.7 = f32[64]{0:T(128)S(1)} all-reduce(f32[64]{0:T(128)S(1)} %get-tuple-element.20), channel_id=1, replica_groups=mesh['groups'=2,'cls'=4,'img'=4] {'cls'}, use_global_device_ids=true, to_apply=%region_3.4 | all-reduce | flops 64 | bytes 512 | tf_op jit(solution)/shard_map/pmax | solution.py:78
  128.4 0.1 exponential_reduce_fusion
  128.6 10.1 %psum.7 = f32[64]{0:T(128)S(1)} all-reduce(f32[64]{0:T(128)S(1)} %get-tuple-element.10), channel_id=1, replica_groups=mesh['groups'=2,'cls'=4,'img'=4] {'cls'}, use_global_device_ids=true, to_apply=%region_5.6 | all-reduce | flops 64 | bytes 512 | tf_op jit(solution)/shard_map/psum | solution.py:79
  138.7 0.1 fusion.16
  138.8 11.4 %fusion = f32[24,32,2,4608]{3,1,2,0:T(8,128)} fusion(bf16[8,2,8,4608]{3,2,1,0:T(8,128)(2,1)S(1)} %bitcast.69, f32[64,24,32]{0,2,1:T(8,128)S(1)} %get-tuple-element.21, f32[64]{0:T(128)S(1)} %log_add_fusion), kind=kOutput, calls=%fused_computation.9 | convolution fusion | flops 906067968 | bytes 29688064 | tf_op jit(solution)/shard_map/dot_general | solution.py:90
  150.2 0.1 fusion.32
  150.4 1.6 fusion.7
  152.0 0.0 reduce-scatter.3.cloned.1.call-start
  152.0 10.9 %add_reduce_fusion = (f32[32,4608]{1,0:T(8,128)S(1)}, f32[32,4608]{1,0:T(8,128)S(1)}) fusion(f32[24,32,2,4608]{3,1,2,0:T(8,128)} %fusion, f32[24,4608]{1,0:T(8,128)} %copy-done.2, f32[24,4608]{1,0:T(8,128)S(1)} %get-tuple-element.16), kind=kLoop, calls=%fused_computation.4 | loop fusion | flops 28016640 | bytes 30375936 | tf_op jit(solution)/shard_map/reduce_sum | solution.py:99
  163.0 1.1 pad_maximum_fusion.1
  164.1 0.6 add_subtract_fusion
  164.7 7.7 %reduce-scatter.5.cloned.1.call-done = f32[32,1152]{1,0:T(8,128)} async-done(((f32[32,4608]{1,0:T(8,128)}), f32[32,1152]{1,0:T(8,128)}) %reduce-scatter.5.cloned.1.call-update) | async-done | bytes 147472 | tf_op jit(solution)/shard_map/reduce_scatter | solution.py:105
  172.4 0.9 broadcast_add_fusion
  173.3 27.4 %reduce-scatter.3.cloned.1.call-done = f32[32,2,1152]{2,0,1:T(8,128)} async-done(((f32[32,2,4608]{2,0,1:T(8,128)}), f32[32,2,1152]{2,0,1:T(8,128)}) %reduce-scatter.3.cloned.1.call-update) | async-done | bytes 294928 | tf_op jit(solution)/shard_map/reduce_scatter | solution.py:104
  200.7 1.0 broadcast_divide_fusion
  201.7 0.9 copy.20
  (19 shorter events, 0.2 us)
Async XLA Ops:
  7.2 104.9 %all-gather.2.cloned.1.call-start = ((), (), s32[]{:S(2)}) async-start(), calls=%async_computation.2 | async-start | bytes 1474560 | tf_op jit(solution)/shard_map/all_gather | solution.py:69
  7.9 77.5 %collective-permute-start = (bf16[16,64]{1,0:T(8,128)(2,1)S(1)}, bf16[16,64]{1,0:T(8,128)(2,1)S(1)}, u32[]{:S(2)}, u32[]{:S(2)}) collective-permute-start(bf16[16,64]{1,0:T(8,128)(2,1)S(1)} %convert_convert_fusion), channel_id=1, source_target_pairs={{0,4},{4,0},{8,12},{12,8},{1,5},{5,1},{9,13},{13,9},{2,6},{6,2},{1... | collective-permute-start | bytes 6152 | tf_op jit(solution)/shard_map/ppermute | solution.py:14
  14.8 157.6 %reduce-scatter.5.cloned.1.call-start = ((), (), s32[]{:S(2)}) async-start(), calls=%async_computation.4 | async-start | bytes 737280 | tf_op jit(solution)/shard_map/reduce_scatter | solution.py:105
  19.7 30.8 %copy-start.2 = (f32[24,4608]{1,0:T(8,128)}, f32[24,4608]{1,0:T(8,128)S(1)}, u32[]{:S(2)}) copy-start(f32[24,4608]{1,0:T(8,128)S(1)} %get-tuple-element.17) | copy-start | bytes 1327108
  50.6 37.6 %copy-start = (f32[64,4608]{1,0:T(8,128)S(1)}, f32[64,4608]{1,0:T(8,128)}, u32[]{:S(2)}) copy-start(f32[64,4608]{1,0:T(8,128)} %param.8) | copy-start | bytes 3538948
  50.6 37.6 %copy-start.3 = (f32[4608]{0:T(1024)S(1)}, f32[4608]{0:T(1024)}, u32[]{:S(2)}) copy-start(f32[4608]{0:T(1024)} %param.9) | copy-start | bytes 55300
  85.5 26.4 %collective-permute-start.1 = (bf16[32,64]{1,0:T(8,128)(2,1)S(1)}, bf16[32,64]{1,0:T(8,128)(2,1)S(1)}, u32[]{:S(2)}, u32[]{:S(2)}) collective-permute-start(bf16[32,64]{1,0:T(8,128)(2,1)S(1)} %maximum_select_fusion.1), channel_id=1, source_target_pairs={{0,8},{4,12},{8,0},{12,4},{1,9},{5,13},{9,1},{13,5},{2,10},{6,14},... | collective-permute-start | bytes 12296 | tf_op jit(solution)/shard_map/ppermute | solution.py:14
  112.1 26.7 %copy-start.1 = (bf16[64,9216]{1,0:T(8,128)(2,1)S(1)}, bf16[64,9216]{1,0:T(8,128)(2,1)}, u32[]{:S(2)}) copy-start(bf16[64,9216]{1,0:T(8,128)(2,1)} %all-gather.2.cloned.1.call-done) | copy-start | bytes 3538948
  152.0 48.8 %reduce-scatter.3.cloned.1.call-start = ((), (), s32[]{:S(2)}) async-start(), calls=%async_computation.3 | async-start | bytes 1474560 | tf_op jit(solution)/shard_map/reduce_scatter | solution.py:104
Sparse Core Ops, SparseCore 0:
  14.9 30.6 all-gather.1
  152.1 20.2 reduce-scatter.4
  175.0 25.7 reduce-scatter.2
